TPU v7x, 512 devices: a whole 4x8x8 slice. The times are simulated.
512 devices in a mesh: doc: 4 (over x), topic: 16 (over z, core), vocab: 8 (over y).
Axes of the slice: x: 4, y: 8, z: 8, core: 2. Of those that a mesh axis runs over, the one named last changes fastest.
Arguments:
- doc_topics: bfloat16 [2048, 16384], P('doc', 'topic'), may hold values from 0 to 1, as said below
- word_logits: bfloat16 [2048, 16384], P('vocab', 'topic'), may hold values from -6 to 11
- log_norm: float32 [16384], P('topic'), may hold values from 12 to 16
- tile_doc: int32 [512], P(('doc', 'vocab')), may hold values from 0 to 3, as said below
- tile_word: int32 [512], P(('doc', 'vocab')), may hold values from 0 to 3
- word_counts: int32 [512, 64, 128], P(('doc', 'vocab')), may hold values from 0 to 3, as said below
Outputs:
- doc_topic_grad: float32 [2048, 16384], P('doc', ('topic', 'vocab'))
- word_logit_grad: bfloat16 [2048, 16384], P('vocab', 'topic')
Inputs may be any that keep to these rules, and one draw needn't show every extreme that they name: `doc_topics`: each document's row is a softmax over the 16384 topics. Within the 16 slots of one doc and vocab index pair no (tile_doc, tile_word) pair repeats. `word_counts`: A slot whose counts are all zero is empty; occupied slots come first in each pair's list, and in every draw some pair has all 16 slots occupied.
All inputs are finite; a program needn't handle non-finite values.
Results may differ from a plain program's by a relative error of at most 0.018.
Values may be sent and summed in bfloat16 or wider, within the bound.
A program may use at most 64 MiB of HBM per device.

v0:
```python
import jax
import jax.numpy as jnp
from jax import lax
from jax.sharding import PartitionSpec as P

tiles_per_step = 8


def on_device(doc_topics, word_logits, log_norm, tile_doc, tile_word, word_counts):
    tile_total, word_span, doc_span = word_counts.shape
    topic_width = doc_topics.shape[1]
    word_prob = jnp.exp(word_logits.astype(jnp.float32) - log_norm[None, :]).astype(jnp.bfloat16)
    topic_blocks = doc_topics.reshape(-1, doc_span, topic_width)
    prob_blocks = word_prob.reshape(-1, word_span, topic_width)
    doc_rows = topic_blocks[tile_doc]
    word_rows = prob_blocks[tile_word]
    word_part = word_rows
    doc_part = doc_rows
    rate_full = lax.psum(
        jnp.einsum("gwk,gdk->gwd", word_part, doc_part, preferred_element_type=jnp.float32).astype(
            jnp.bfloat16
        ),
        "topic",
    ).astype(jnp.float32)
    ratios = (word_counts.astype(jnp.float32) / (word_span * rate_full)).astype(jnp.bfloat16)

    def accumulate(state_pair, group_index):
        theta_acc, beta_acc = state_pair
        first_row = group_index * tiles_per_step
        ratio_part = lax.dynamic_slice_in_dim(ratios, first_row, tiles_per_step, 0)
        word_part = lax.dynamic_slice_in_dim(word_rows, first_row, tiles_per_step, 0)
        doc_part = lax.dynamic_slice_in_dim(doc_rows, first_row, tiles_per_step, 0)
        doc_index = lax.dynamic_slice_in_dim(tile_doc, first_row, tiles_per_step, 0)
        word_index = lax.dynamic_slice_in_dim(tile_word, first_row, tiles_per_step, 0)
        toward_theta = jnp.einsum(
            "gwd,gwk->gdk", ratio_part, word_part, preferred_element_type=jnp.float32
        )
        toward_beta = jnp.einsum(
            "gwd,gdk->gwk", ratio_part, doc_part, preferred_element_type=jnp.float32
        )
        return (
            (theta_acc.at[doc_index].add(toward_theta), beta_acc.at[word_index].add(toward_beta)),
            None,
        )

    initial = (
        jnp.zeros(topic_blocks.shape, jnp.float32),
        jnp.zeros(prob_blocks.shape, jnp.float32),
    )
    steps_all = jnp.arange(tile_total // tiles_per_step, dtype=jnp.int32)
    (theta_acc, beta_acc), _ = lax.scan(accumulate, initial, steps_all)
    theta_term = -theta_acc.reshape(doc_topics.shape)
    doc_topic_grad = lax.psum_scatter(
        theta_term.astype(jnp.bfloat16), "vocab", scatter_dimension=1, tiled=True
    ).astype(jnp.float32)
    beta_term = -word_prob.astype(jnp.float32) * beta_acc.reshape(word_prob.shape)
    word_logit_grad = lax.psum(beta_term.astype(jnp.bfloat16), "doc")
    return (doc_topic_grad, word_logit_grad)


def solution(mesh):
    placed = (
        P("doc", "topic"),
        P("vocab", "topic"),
        P("topic"),
        P(("doc", "vocab")),
        P(("doc", "vocab")),
        P(("doc", "vocab"), None, None),
    )
    return jax.shard_map(
        on_device,
        mesh=mesh,
        in_specs=placed,
        out_specs=(P("doc", ("topic", "vocab")), P("vocab", "topic")),
        check_vma=False,
    )
```

profile of v0, /device:TPU:8, one launch (start us, length us, event | category | flops | bytes accessed | tf_op | source)
XLA Modules:
  0.0 288.9 jit_solution(454875629672425945)
XLA Ops:
  7.2 0.0 copy-start
  7.2 0.0 all-reduce.3.cloned.1.call-start
  7.2 0.7 compare_select_fusion.2
  8.0 0.7 compare_select_fusion.3
  8.6 2.0 exponential_convert_fusion
  10.6 1.7 gather_fusion
  12.4 0.0 copy-done
  12.4 0.0 copy-start.2
  12.4 2.8 gather_fusion.1
  15.1 0.0 copy-done.2
  15.1 4.4 %convolution_convert_fusion = bf16[16,64,128]{2,1,0:T(8,128)(2,1)} fusion(bf16[16,64,1024]{2,1,0:T(8,128)(2,1)S(1)} %gather_fusion, bf16[16,128,1024]{2,1,0:T(8,128)(2,1)} %gather_fusion.1), kind=kOutput, calls=%fused_computation.15 | convolution fusion | flops 268566528 | bytes 6553600 | tf_op jit(solution)/shard_map/gwk,gdk->gwd/dot_general | solution.py:20
  19.6 0.0 all-reduce.3.cloned.1.call-update
  19.6 0.0 reduce-scatter.4.cloned.1.call-start
  19.7 0.0 copy-start.5
  19.7 0.0 copy-start.6
  19.7 119.4 %all-reduce.3.cloned.1.call-done = bf16[16,64,128]{2,1,0:T(8,128)(2,1)} async-done(((bf16[16,64,128]{2,1,0:T(8,128)(2,1)}), bf16[16,64,128]{2,1,0:T(8,128)(2,1)}) %all-reduce.3.cloned.1.call-update) | async-done | bytes 262160 | tf_op jit(solution)/shard_map/psum | solution.py:19
  139.1 1.2 divide_convert_fusion
  140.3 1.1 broadcast_in_dim.20
  141.4 0.2 broadcast_in_dim.19
  141.7 0.0 copy-done.5
  141.7 0.0 copy-done.6
  141.7 38.2 %while.12 = (s32[]{:T(128)}, f32[4,128,1024]{2,1,0:T(8,128)S(1)}, f32[4,64,1024]{2,1,0:T(8,128)}, s32[2]{0:T(128)S(1)}, s32[16]{0:T(128)S(1)}, /*index=5*/bf16[1...) while((s32[]{:T(128)}, f32[4,128,1024]{2,1,0:T(8,128)S(1)}, ...), condition=%wide.region_4.5_spmd, body=%wide.region_1.4_spmd.sunk | while | flops 270008384 | bytes 28576132 | solution.py:51
  141.7 0.6 dynamic_slice.40
  143.0 0.1 compare_select_fusion.5
  143.0 3.3 %fusion.22 = f32[8,64,1024]{2,1,0:T(8,128)} fusion(bf16[16,128,1024]{2,1,0:T(8,128)(2,1)} %get-tuple-element.165, s32[]{:T(128)S(6)} %select_n.28, bf16[16,64,128]{2,1,0:T(8,128)(2,1)S(1)} %get-tuple-element.162), kind=kOutput, calls=%fused_computation.4.clone.1 | convolution fusion | flops 134217728 | bytes 4326400 | tf_op jit(solution)/shard_map/while/body/eval_jaxpr/gwd,gdk->gwk/dot_general | solution.py:38
  146.4 4.8 %scatter_fusion.1 = f32[4,64,1024]{2,1,0:T(8,128)} fusion(f32[4,64,1024]{2,1,0:T(8,128)} %get-tuple-element.146, s32[8]{0:T(128)S(1)} %get-tuple-element.130, f32[8,64,1024]{2,1,0:T(8,128)} %fusion.22), kind=kCustom, calls=%fused_computation.3.clone.1 | custom fusion | flops 524288 | bytes 6291488 | tf_op jit(solution)/shard_map/while/body/eval_jaxpr/scatter-add | solution.py:42
  151.1 3.9 %fusion.21 = f32[8,128,1024]{2,1,0:T(8,128)} fusion(bf16[16,64,1024]{2,1,0:T(8,128)(2,1)} %get-tuple-element.163, s32[]{:T(128)S(6)} %select_n.28, bf16[16,64,128]{2,1,0:T(8,128)(2,1)S(1)} %get-tuple-element.162), kind=kOutput, calls=%fused_computation.6.clone.1 | convolution fusion | flops 134217728 | bytes 5374976 | tf_op jit(solution)/shard_map/while/body/eval_jaxpr/gwd,gwk->gdk/dot_general | solution.py:35
  155.1 5.7 %scatter_fusion = f32[4,128,1024]{2,1,0:T(8,128)S(1)} fusion(f32[4,128,1024]{2,1,0:T(8,128)S(1)} %get-tuple-element.145, s32[8]{0:T(128)S(1)} %get-tuple-element.129, f32[8,128,1024]{2,1,0:T(8,128)} %fusion.21), kind=kCustom, calls=%fused_computation.2.clone.1 | custom fusion | flops 1048576 | bytes 12582944 | tf_op jit(solution)/shard_map/while/body/eval_jaxpr/scatter-add | solution.py:42
  160.8 0.6 dynamic_slice.40
  162.1 0.1 compare_select_fusion.5
  162.2 3.3 %fusion.22 = f32[8,64,1024]{2,1,0:T(8,128)} fusion(bf16[16,128,1024]{2,1,0:T(8,128)(2,1)} %get-tuple-element.165, s32[]{:T(128)S(6)} %select_n.28, bf16[16,64,128]{2,1,0:T(8,128)(2,1)S(1)} %get-tuple-element.162), kind=kOutput, calls=%fused_computation.4.clone.1 | convolution fusion | flops 134217728 | bytes 4326400 | tf_op jit(solution)/shard_map/while/body/eval_jaxpr/gwd,gdk->gwk/dot_general | solution.py:38
  165.5 4.8 %scatter_fusion.1 = f32[4,64,1024]{2,1,0:T(8,128)} fusion(f32[4,64,1024]{2,1,0:T(8,128)} %get-tuple-element.146, s32[8]{0:T(128)S(1)} %get-tuple-element.130, f32[8,64,1024]{2,1,0:T(8,128)} %fusion.22), kind=kCustom, calls=%fused_computation.3.clone.1 | custom fusion | flops 524288 | bytes 6291488 | tf_op jit(solution)/shard_map/while/body/eval_jaxpr/scatter-add | solution.py:42
  170.3 3.9 %fusion.21 = f32[8,128,1024]{2,1,0:T(8,128)} fusion(bf16[16,64,1024]{2,1,0:T(8,128)(2,1)} %get-tuple-element.163, s32[]{:T(128)S(6)} %select_n.28, bf16[16,64,128]{2,1,0:T(8,128)(2,1)S(1)} %get-tuple-element.162), kind=kOutput, calls=%fused_computation.6.clone.1 | convolution fusion | flops 134217728 | bytes 5374976 | tf_op jit(solution)/shard_map/while/body/eval_jaxpr/gwd,gwk->gdk/dot_general | solution.py:35
  174.2 5.7 %scatter_fusion = f32[4,128,1024]{2,1,0:T(8,128)S(1)} fusion(f32[4,128,1024]{2,1,0:T(8,128)S(1)} %get-tuple-element.145, s32[8]{0:T(128)S(1)} %get-tuple-element.129, f32[8,128,1024]{2,1,0:T(8,128)} %fusion.21), kind=kCustom, calls=%fused_computation.2.clone.1 | custom fusion | flops 1048576 | bytes 12582944 | tf_op jit(solution)/shard_map/while/body/eval_jaxpr/scatter-add | solution.py:42
  180.0 1.3 negate_convert_fusion
  181.2 2.4 copy.8
  183.6 0.0 reduce-scatter.4.cloned.1.call-update
  183.6 0.0 all-reduce.5.cloned.1.call-start
  183.7 0.0 copy-done.1
  183.7 0.0 copy-done.3
  183.7 0.0 copy-done.4
  183.7 1.0 fusion.8
  184.7 0.0 all-reduce.5.cloned.1.call-update
  184.8 39.5 %reduce-scatter.4.cloned.1.call-done = bf16[128,512]{1,0:T(8,128)(2,1)} async-done(((bf16[1024,512]{1,0:T(8,128)(2,1)}), bf16[128,512]{1,0:T(8,128)(2,1)}) %reduce-scatter.4.cloned.1.call-update) | async-done | bytes 131088
  224.3 1.0 copy.9
  225.3 0.7 convert_element_type.41
  226.0 54.5 %all-reduce.5.cloned.1.call-done = bf16[256,1024]{1,0:T(8,128)(2,1)} async-done(((bf16[256,1024]{1,0:T(8,128)(2,1)}), bf16[256,1024]{1,0:T(8,128)(2,1)}) %all-reduce.5.cloned.1.call-update) | async-done | bytes 524304 | tf_op jit(solution)/shard_map/psum | solution.py:57
  280.5 1.9 copy.23
  (6 shorter events, 0.0 us)
Async XLA Ops:
  7.2 5.2 %copy-start = (bf16[512,1024]{1,0:T(8,128)(2,1)S(1)}, bf16[512,1024]{1,0:T(8,128)(2,1)}, u32[]{:S(2)}) copy-start(bf16[512,1024]{1,0:T(8,128)(2,1)} %param.8) | copy-start | bytes 3145732
  7.2 131.9 %all-reduce.3.cloned.1.call-start = ((), (), s32[]{:S(2)}) async-start(), calls=%async_computation.1 | async-start | bytes 524288 | tf_op jit(solution)/shard_map/psum | solution.py:19
  12.4 2.8 copy-start.2
  19.6 204.7 %reduce-scatter.4.cloned.1.call-start = ((), (), s32[]{:S(2)}) async-start(), calls=%async_computation.3 | async-start | bytes 1179648
  19.7 122.0 %copy-start.5 = (s32[16]{0:T(128)S(1)}, s32[16]{0:T(128)}, u32[]{:S(2)}) copy-start(s32[16]{0:T(128)} %param.12) | copy-start | bytes 196
  19.7 122.0 %copy-start.6 = (s32[16]{0:T(128)S(1)}, s32[16]{0:T(128)}, u32[]{:S(2)}) copy-start(s32[16]{0:T(128)} %param.11) | copy-start | bytes 196
  181.2 2.5 copy-start.1
  181.2 2.5 copy-start.3
  181.2 2.5 copy-start.4
  183.6 96.8 %all-reduce.5.cloned.1.call-start = ((), (), s32[]{:S(2)}) async-start(), calls=%async_computation.2 | async-start | bytes 1048576 | tf_op jit(solution)/shard_map/psum | solution.py:57
Sparse Core Ops, SparseCore 0:
  19.7 119.3 all-reduce.2
  183.8 40.4 reduce-scatter.3
  227.3 53.1 all-reduce.4
where the time goes:
time: 290 us; the launch traced here: 289 us
  waiting for transfers between devices  213 us (73%)
  other arithmetic  28.8 us (10%)
  matrix products  19 us (7%)
  between operations  13.9 us (5%)
  local copies, waits for them, and re-layouts  12.3 us (4%)
    psum x1, waiting for transfers between devices, on_device(): lax.psum(jnp.einsum('gwk,gdk->gwd', word_part, doc_part, preferred_elemen...  119 us
    psum x1, waiting for transfers between devices, on_device(): word_logit_grad = lax.psum(beta_term.astype(jnp.bfloat16), 'doc')  54.5 us
    unnamed x4, waiting for transfers between devices  39.6 us
    scatter-add x2, other arithmetic, accumulate(): theta_acc.at[doc_index].add(toward_theta)  11.5 us
    scatter-add x2, other arithmetic, accumulate(): beta_acc.at[word_index].add(toward_beta)  9.54 us
    dot_general x2, matrix products, accumulate(): jnp.einsum('gwd,gwk->gdk', ratio_part, word_part, preferred_element_type=...  7.89 us
    dot_general x2, matrix products, accumulate(): jnp.einsum('gwd,gdk->gwk', ratio_part, doc_part, preferred_element_type=j...  6.67 us
  transfers between devices with their start and end apart: 3, of which 3 were waited for; matrix products, arithmetic and copies ran while one was open for 1% of the time, Pallas kernels for 0%

commit v1 on v0

--- a/solution.py
+++ b/solution.py
@@ -16,11 +16,14 @@
     word_rows = prob_blocks[tile_word]
     word_part = word_rows
     doc_part = doc_rows
-    rate_full = lax.psum(
-        jnp.einsum("gwk,gdk->gwd", word_part, doc_part, preferred_element_type=jnp.float32).astype(
-            jnp.bfloat16
+    rate_full = jnp.sum(
+        lax.all_gather(
+            jnp.einsum(
+                "gwk,gdk->gwd", word_part, doc_part, preferred_element_type=jnp.float32
+            ).astype(jnp.bfloat16),
+            "topic",
         ),
-        "topic",
+        axis=0,
     ).astype(jnp.float32)
     ratios = (word_counts.astype(jnp.float32) / (word_span * rate_full)).astype(jnp.bfloat16)
 

time: 290 us -> 221 us (0.76)
  waiting for transfers between devices: 213 us -> 143 us
    psum x1 -> x0, waiting for transfers between devices: 119 us -> none  [on_device(): lax.psum(jnp.einsum('gwk,gdk->gwd', word_part, doc_part, preferred_elemen...]
    all_gather x0 -> x1, waiting for transfers between devices: none -> 50.4 us  [on_device(): lax.all_gather(jnp.einsum('gwk,gdk->gwd', word_part, doc_part, preferred_...]
    reduce_sum x0 -> x1, other arithmetic: none -> 3.18 us  [on_device(): jnp.sum(lax.all_gather(jnp.einsum('gwk,gdk->gwd', word_part, doc_part, pr...]
where the time goes in v1:
time: 221 us; the launch traced here: 220 us
  waiting for transfers between devices  143 us (65%)
  other arithmetic  30.9 us (14%)
  matrix products  19 us (9%)
  between operations  13.9 us (6%)
  local copies, waits for them, and re-layouts  12.3 us (6%)
    psum x1, waiting for transfers between devices, on_device(): word_logit_grad = lax.psum(beta_term.astype(jnp.bfloat16), 'doc')  54.5 us
    all_gather x1, waiting for transfers between devices, on_device(): lax.all_gather(jnp.einsum('gwk,gdk->gwd', word_part, doc_part, preferred_...  50.4 us
    unnamed x4, waiting for transfers between devices  37.7 us
    scatter-add x2, other arithmetic, accumulate(): theta_acc.at[doc_index].add(toward_theta)  11.5 us
    scatter-add x2, other arithmetic, accumulate(): beta_acc.at[word_index].add(toward_beta)  9.54 us
    dot_general x2, matrix products, accumulate(): jnp.einsum('gwd,gwk->gdk', ratio_part, word_part, preferred_element_type=...  7.88 us
    dot_general x2, matrix products, accumulate(): jnp.einsum('gwd,gdk->gwk', ratio_part, doc_part, preferred_element_type=j...  6.69 us
    unnamed x19, local copies, waits for them, and re-layouts  5.32 us
  transfers between devices with their start and end apart: 3, of which 3 were waited for; matrix products, arithmetic and copies ran while one was open for 1% of the time, Pallas kernels for 0%

profile of v1, /device:TPU:8, one launch (start us, length us, event | category | flops | bytes accessed | tf_op | source)
XLA Modules:
  0.0 220.1 jit_solution(5261364690088767394)
XLA Ops:
  7.2 0.0 copy-start
  7.2 0.0 all-gather.3.cloned.1.call-start
  7.2 0.7 compare_select_fusion.2
  8.0 0.7 compare_select_fusion.3
  8.6 2.0 exponential_convert_fusion
  10.6 1.7 gather_fusion
  12.4 0.0 copy-done
  12.4 0.0 copy-start.2
  12.4 2.8 %gather_fusion.1 = bf16[16,128,1024]{2,1,0:T(8,128)(2,1)} fusion(bf16[4,128,1024]{2,1,0:T(8,128)(2,1)S(1)} %bitcast.15, s32[1024]{0:T(1024)S(1)} %pad_clamp_fusion), kind=kCustom, calls=%fused_computation.1 | custom fusion | bytes 8388672 | tf_op jit(solution)/shard_map/gather | solution.py:15
  15.1 0.0 copy-done.2
  15.1 4.4 %convolution_convert_fusion = bf16[16,64,128]{2,1,0:T(8,128)(2,1)} fusion(bf16[16,64,1024]{2,1,0:T(8,128)(2,1)S(1)} %gather_fusion, bf16[16,128,1024]{2,1,0:T(8,128)(2,1)} %gather_fusion.1), kind=kOutput, calls=%fused_computation.15 | convolution fusion | flops 268566528 | bytes 6553600 | tf_op jit(solution)/shard_map/gwk,gdk->gwd/dot_general | solution.py:21
  19.6 0.0 all-gather.3.cloned.1.call-update
  19.6 0.0 reduce-scatter.4.cloned.1.call-start
  19.7 50.4 %all-gather.3.cloned.1.call-done = bf16[256,64,128]{2,1,0:T(8,128)(2,1)} async-done(((bf16[16,64,128]{2,1,0:T(8,128)(2,1)}), bf16[256,64,128]{2,1,0:T(8,128)(2,1)}) %all-gather.3.cloned.1.call-update) | async-done | bytes 4194320 | tf_op jit(solution)/shard_map/all_gather | solution.py:20
  70.0 3.2 %reduce_sum.12 = bf16[16,64,128]{2,1,0:T(8,128)(2,1)S(1)} reduce(bf16[16,16,64,128]{3,2,1,0:T(8,128)(2,1)} %bitcast.18, bf16[]{:T(256)} %constant.7.clone.1), dimensions={0}, to_apply=%region_0.0 | reduce | flops 1966080 | bytes 4456450 | tf_op jit(solution)/shard_map/reduce_sum | solution.py:19
  73.2 0.0 copy-done.4
  73.2 0.0 copy-start.6
  73.2 0.0 copy-start.7
  73.2 0.1 divide_convert_fusion
  73.4 1.1 broadcast_in_dim.20
  74.5 0.2 broadcast_in_dim.19
  74.7 0.0 copy-done.6
  74.7 0.0 copy-done.7
  74.7 38.3 %while.12 = (s32[]{:T(128)}, f32[4,128,1024]{2,1,0:T(8,128)S(1)}, f32[4,64,1024]{2,1,0:T(8,128)}, s32[2]{0:T(128)S(1)}, s32[16]{0:T(128)S(1)}, /*index=5*/bf16[1...) while((s32[]{:T(128)}, f32[4,128,1024]{2,1,0:T(8,128)S(1)}, ...), condition=%wide.region_4.5_spmd, body=%wide.region_1.4_spmd.sunk | while | flops 270008384 | bytes 28576132 | solution.py:54
  74.7 0.6 dynamic_slice.40
  76.0 0.1 compare_select_fusion.5
  76.1 3.3 %fusion.22 = f32[8,64,1024]{2,1,0:T(8,128)} fusion(bf16[16,128,1024]{2,1,0:T(8,128)(2,1)} %get-tuple-element.165, s32[]{:T(128)S(6)} %select_n.28, bf16[16,64,128]{2,1,0:T(8,128)(2,1)S(1)} %get-tuple-element.162), kind=kOutput, calls=%fused_computation.4.clone.1 | convolution fusion | flops 134217728 | bytes 4326400 | tf_op jit(solution)/shard_map/while/body/eval_jaxpr/gwd,gdk->gwk/dot_general | solution.py:41
  79.4 4.8 %scatter_fusion.1 = f32[4,64,1024]{2,1,0:T(8,128)} fusion(f32[4,64,1024]{2,1,0:T(8,128)} %get-tuple-element.146, s32[8]{0:T(128)S(1)} %get-tuple-element.130, f32[8,64,1024]{2,1,0:T(8,128)} %fusion.22), kind=kCustom, calls=%fused_computation.3.clone.1 | custom fusion | flops 524288 | bytes 6291488 | tf_op jit(solution)/shard_map/while/body/eval_jaxpr/scatter-add | solution.py:45
  84.2 3.9 %fusion.21 = f32[8,128,1024]{2,1,0:T(8,128)} fusion(bf16[16,64,1024]{2,1,0:T(8,128)(2,1)} %get-tuple-element.163, s32[]{:T(128)S(6)} %select_n.28, bf16[16,64,128]{2,1,0:T(8,128)(2,1)S(1)} %get-tuple-element.162), kind=kOutput, calls=%fused_computation.6.clone.1 | convolution fusion | flops 134217728 | bytes 5374976 | tf_op jit(solution)/shard_map/while/body/eval_jaxpr/gwd,gwk->gdk/dot_general | solution.py:38
  88.1 5.7 %scatter_fusion = f32[4,128,1024]{2,1,0:T(8,128)S(1)} fusion(f32[4,128,1024]{2,1,0:T(8,128)S(1)} %get-tuple-element.145, s32[8]{0:T(128)S(1)} %get-tuple-element.129, f32[8,128,1024]{2,1,0:T(8,128)} %fusion.21), kind=kCustom, calls=%fused_computation.2.clone.1 | custom fusion | flops 1048576 | bytes 12582944 | tf_op jit(solution)/shard_map/while/body/eval_jaxpr/scatter-add | solution.py:45
  93.9 0.6 dynamic_slice.40
  95.1 0.1 compare_select_fusion.5
  95.2 3.3 %fusion.22 = f32[8,64,1024]{2,1,0:T(8,128)} fusion(bf16[16,128,1024]{2,1,0:T(8,128)(2,1)} %get-tuple-element.165, s32[]{:T(128)S(6)} %select_n.28, bf16[16,64,128]{2,1,0:T(8,128)(2,1)S(1)} %get-tuple-element.162), kind=kOutput, calls=%fused_computation.4.clone.1 | convolution fusion | flops 134217728 | bytes 4326400 | tf_op jit(solution)/shard_map/while/body/eval_jaxpr/gwd,gdk->gwk/dot_general | solution.py:41
  98.5 4.8 %scatter_fusion.1 = f32[4,64,1024]{2,1,0:T(8,128)} fusion(f32[4,64,1024]{2,1,0:T(8,128)} %get-tuple-element.146, s32[8]{0:T(128)S(1)} %get-tuple-element.130, f32[8,64,1024]{2,1,0:T(8,128)} %fusion.22), kind=kCustom, calls=%fused_computation.3.clone.1 | custom fusion | flops 524288 | bytes 6291488 | tf_op jit(solution)/shard_map/while/body/eval_jaxpr/scatter-add | solution.py:45
  103.3 3.9 %fusion.21 = f32[8,128,1024]{2,1,0:T(8,128)} fusion(bf16[16,64,1024]{2,1,0:T(8,128)(2,1)} %get-tuple-element.163, s32[]{:T(128)S(6)} %select_n.28, bf16[16,64,128]{2,1,0:T(8,128)(2,1)S(1)} %get-tuple-element.162), kind=kOutput, calls=%fused_computation.6.clone.1 | convolution fusion | flops 134217728 | bytes 5374976 | tf_op jit(solution)/shard_map/while/body/eval_jaxpr/gwd,gwk->gdk/dot_general | solution.py:38
  107.3 5.7 %scatter_fusion = f32[4,128,1024]{2,1,0:T(8,128)S(1)} fusion(f32[4,128,1024]{2,1,0:T(8,128)S(1)} %get-tuple-element.145, s32[8]{0:T(128)S(1)} %get-tuple-element.129, f32[8,128,1024]{2,1,0:T(8,128)} %fusion.21), kind=kCustom, calls=%fused_computation.2.clone.1 | custom fusion | flops 1048576 | bytes 12582944 | tf_op jit(solution)/shard_map/while/body/eval_jaxpr/scatter-add | solution.py:45
  113.0 1.3 negate_convert_fusion
  114.3 2.4 %copy.8 = bf16[512,1024]{0,1:T(8,128)(2,1)} copy(bf16[512,1024]{1,0:T(8,128)(2,1)} %bitcast.17) | data formatting | bytes 2097152
  116.7 0.0 reduce-scatter.4.cloned.1.call-update
  116.7 0.0 all-reduce.2.cloned.1.call-start
  116.7 0.0 copy-done.1
  116.8 1.0 fusion.8
  117.8 0.0 all-reduce.2.cloned.1.call-update
  117.8 37.6 %reduce-scatter.4.cloned.1.call-done = bf16[128,512]{1,0:T(8,128)(2,1)} async-done(((bf16[1024,512]{1,0:T(8,128)(2,1)}), bf16[128,512]{1,0:T(8,128)(2,1)}) %reduce-scatter.4.cloned.1.call-update) | async-done | bytes 131088
  155.5 1.0 copy.9
  156.5 0.7 convert_element_type.43
  157.2 54.5 %all-reduce.2.cloned.1.call-done = bf16[256,1024]{1,0:T(8,128)(2,1)} async-done(((bf16[256,1024]{1,0:T(8,128)(2,1)}), bf16[256,1024]{1,0:T(8,128)(2,1)}) %all-reduce.2.cloned.1.call-update) | async-done | bytes 524304 | tf_op jit(solution)/shard_map/psum | solution.py:60
  211.7 1.9 copy.22
  (9 shorter events, 0.0 us)
Async XLA Ops:
  7.2 5.2 %copy-start = (bf16[512,1024]{1,0:T(8,128)(2,1)S(1)}, bf16[512,1024]{1,0:T(8,128)(2,1)}, u32[]{:S(2)}) copy-start(bf16[512,1024]{1,0:T(8,128)(2,1)} %param.8) | copy-start | bytes 3145732
  7.2 62.8 %all-gather.3.cloned.1.call-start = ((), (), s32[]{:S(2)}) async-start(), calls=%async_computation.2 | async-start | bytes 4456448 | tf_op jit(solution)/shard_map/all_gather | solution.py:20
  12.4 2.8 %copy-start.2 = (bf16[16,64,1024]{2,1,0:T(8,128)(2,1)}, bf16[16,64,1024]{2,1,0:T(8,128)(2,1)S(1)}, u32[]{:S(2)}) copy-start(bf16[16,64,1024]{2,1,0:T(8,128)(2,1)S(1)} %gather_fusion) | copy-start | bytes 6291460
  19.6 135.9 %reduce-scatter.4.cloned.1.call-start = ((), (), s32[]{:S(2)}) async-start(), calls=%async_computation.3 | async-start | bytes 1179648
  70.0 3.2 %copy-start.4 = (s32[16,64,128]{2,1,0:T(8,128)S(1)}, s32[16,64,128]{2,1,0:T(8,128)}, u32[]{:S(2)}) copy-start(s32[16,64,128]{2,1,0:T(8,128)} %param.13) | copy-start | bytes 1572868
  73.2 1.5 copy-start.6
  73.2 1.5 copy-start.7
  114.3 2.5 %copy-start.1 = (f32[4,64,1024]{2,1,0:T(8,128)S(1)}, f32[4,64,1024]{2,1,0:T(8,128)}, u32[]{:S(2)}) copy-start(f32[4,64,1024]{2,1,0:T(8,128)} %get-tuple-element.51) | copy-start | bytes 3145732
  114.3 2.5 %copy-start.3 = (bf16[256,1024]{1,0:T(8,128)(2,1)S(1)}, bf16[256,1024]{1,0:T(8,128)(2,1)}, u32[]{:S(2)}) copy-start(bf16[256,1024]{1,0:T(8,128)(2,1)} %param.9) | copy-start | bytes 1572868
  114.3 2.5 %copy-start.5 = (f32[1024]{0:T(1024)S(1)}, f32[1024]{0:T(1024)}, u32[]{:S(2)}) copy-start(f32[1024]{0:T(1024)} %param.10) | copy-start | bytes 12292
  116.7 95.0 %all-reduce.2.cloned.1.call-start = ((), (), s32[]{:S(2)}) async-start(), calls=%async_computation.1 | async-start | bytes 1048576 | tf_op jit(solution)/shard_map/psum | solution.py:60
Sparse Core Ops, SparseCore 0:
  19.7 50.2 all-gather.2
  116.8 38.6 reduce-scatter.3
  158.4 53.2 all-reduce.1
